TPU v7x, 32 devices: a whole 2x2x4 slice. The times are simulated.
32 devices in a mesh: row: 8 (over y, x, core), col: 4 (over z).
Axes of the slice: x: 2, y: 2, z: 4, core: 2. Of those that a mesh axis runs over, the one named last changes fastest.
Arguments:
- points: bfloat16 [16, 16384], P(None, ('row', 'col')), may hold values from -6 to 6
- spread: bfloat16 [16384], P(('row', 'col')), may hold values from 2 to 12
- vectors: bfloat16 [8, 16384], P(None, ('row', 'col')), may hold values from -6 to 6
Outputs:
- basis: float32 [8, 16384], P(None, ('row', 'col'))
All inputs are finite; a program needn't handle non-finite values.
Results may differ from a plain program's by a relative error of at most 0.012.
Values may be sent and summed in bfloat16 or wider, within the bound.
No kernel may reach another device: no remote copies, remote signals or barrier semaphores. Data moves between devices by JAX's collectives and lax.ppermute only.
A program may use at most 64 MiB of HBM per device.

v0:
```python
import math
import jax
import jax.numpy as jnp
from jax import lax
from jax.sharding import PartitionSpec as P


def squared_norm(pts):
    values = pts.astype(jnp.float32)
    return jnp.sum(values * values, axis=0)


def affinity_block(pts_left, norm_left, scale_left, pts_right, norm_right, scale_right):
    cross = lax.dot_general(
        pts_left, pts_right, (((0,), (0,)), ((), ())), preferred_element_type=jnp.float32
    )
    dist = norm_left[:, None] + norm_right[None, :] - 2.0 * cross
    denom = scale_left.astype(jnp.float32)[:, None] * scale_right.astype(jnp.float32)[None, :]
    return jnp.exp(-dist / denom).astype(jnp.bfloat16)


def with_ones(vecs):
    return jnp.concatenate([vecs, jnp.ones((1,) + vecs.shape[1:], jnp.bfloat16)], axis=0)


def shards(points, spread, vectors):
    n_row = lax.axis_size("row")
    n_col = lax.axis_size("col")
    local = points.shape[1]
    dims = points.shape[0]
    kvec = vectors.shape[0]
    col_pts, col_scale, col_vecs = (
        lax.all_gather(points, "row", axis=1, tiled=True),
        lax.all_gather(spread, "row", axis=0, tiled=True),
        lax.all_gather(vectors, "row", axis=1, tiled=True),
    )
    col_ext = with_ones(col_vecs)
    col_norm = squared_norm(col_pts)
    row_pts, row_scale = (
        lax.all_gather(points, "col", axis=1, tiled=True),
        lax.all_gather(spread, "col", axis=0, tiled=True),
    )
    row_norm = squared_norm(row_pts)
    group = math.gcd(n_col, max(1, 512 // local))
    size = group * local
    nblocks = n_col // group
    pts_blocks = jnp.transpose(row_pts.reshape(dims, nblocks, size), (1, 0, 2))
    norm_blocks = row_norm.reshape(nblocks, size)
    scale_blocks = row_scale.reshape(nblocks, size)

    def one_block(operands):
        pts_blk, norm_blk, scale_blk = operands
        affinity = affinity_block(pts_blk, norm_blk, scale_blk, col_pts, col_norm, col_scale)
        return lax.dot_general(
            col_ext, affinity, (((1,), (1,)), ((), ())), preferred_element_type=jnp.float32
        )

    parts = lax.map(one_block, (pts_blocks, norm_blocks, scale_blocks))
    row_part = jnp.transpose(parts, (1, 0, 2)).reshape(kvec + 1, n_col * local)
    total = lax.psum_scatter(row_part, "col", scatter_dimension=1, tiled=True)
    update = total[:kvec] / total[kvec : kvec + 1]
    gram_local = jnp.sum(update[:, None, :] * update[None, :, :], axis=2)
    gram = lax.psum(gram_local, ("row", "col"))
    lower = jnp.linalg.cholesky(gram)
    solved = lax.linalg.triangular_solve(lower, update, left_side=True, lower=True)
    count = local * n_row * n_col
    return jnp.sqrt(jnp.float32(count)) * solved


def solution(mesh):
    in_specs = (P(None, ("row", "col")), P(("row", "col")), P(None, ("row", "col")))
    out_specs = P(None, ("row", "col"))
    return jax.shard_map(shards, mesh=mesh, in_specs=in_specs, out_specs=out_specs, check_vma=False)
```

profile of v0, /device:TPU:10, one launch (start us, length us, event | category | flops | bytes accessed | tf_op | source)
XLA Modules:
  0.0 145.8 jit_solution(7254464226759847502)
XLA Ops:
  6.5 0.0 reduce-scatter.2.cloned.1.call-start
  6.5 13.7 %all_gather.15 = bf16[16,2048]{1,0:T(8,128)(2,1)S(1)} all-gather(bf16[16,512]{1,0:T(8,128)(2,1)} %param.5), channel_id=1, replica_groups=mesh['row'=8,'col'=4] {'col'}, dimensions={1}, use_global_device_ids=true | all-gather | bytes 81920 | tf_op jit(solution)/shard_map/all_gather | solution.py:40
  20.3 9.2 %all_gather.16 = bf16[16,4096]{1,0:T(8,128)(2,1)S(1)} all-gather(bf16[16,512]{1,0:T(8,128)(2,1)} %param.5), channel_id=1, replica_groups=mesh['row'=8,'col'=4] {'row'}, dimensions={1}, use_global_device_ids=true | all-gather | bytes 147456 | tf_op jit(solution)/shard_map/all_gather | solution.py:33
  29.5 0.0 copy-start.1
  29.6 0.6 copy-done.1
  30.2 8.1 %all-gather.1 = bf16[8,1,512]{2,1,0:T(2,128)(2,1)S(1)} all-gather(bf16[1,1,512]{2,1,0:T(2,128)(2,1)S(1)} %reshape.41), channel_id=1, replica_groups=mesh['row'=8,'col'=4] {'row'}, dimensions={0}, use_global_device_ids=true | all-gather | bytes 9216 | tf_op jit(solution)/shard_map/all_gather | solution.py:34
  38.3 11.9 %all-gather = bf16[4,1,512]{2,1,0:T(2,128)(2,1)S(1)} all-gather(bf16[1,1,512]{2,1,0:T(2,128)(2,1)S(1)} %reshape.41), channel_id=1, replica_groups=mesh['row'=8,'col'=4] {'col'}, dimensions={0}, use_global_device_ids=true | all-gather | bytes 5120 | tf_op jit(solution)/shard_map/all_gather | solution.py:41
  50.2 0.0 copy-start
  50.3 0.1 multiply_reduce_fusion
  50.3 0.1 reduce.6
  50.4 0.5 copy-done
  50.9 9.0 %all_gather.19 = bf16[8,4096]{1,0:T(8,128)(2,1)S(1)} all-gather(bf16[8,512]{1,0:T(8,128)(2,1)S(1)} %copy-done), channel_id=1, replica_groups=mesh['row'=8,'col'=4] {'row'}, dimensions={1}, use_global_device_ids=true | all-gather | bytes 73728 | tf_op jit(solution)/shard_map/all_gather | solution.py:35
  60.0 14.6 %while.10 = (s32[]{:T(128)}, f32[4,9,512]{2,1,0:T(8,128)S(1)}, f32[4,512]{1,0:T(4,128)S(1)}, f32[4096]{0:T(1024)S(1)}, bf16[4,16,512]{2,1,0:T(8,128)(2,1)S(1)}, ...) while((s32[]{:T(128)}, f32[4,9,512]{2,1,0:T(8,128)S(1)}, ...), condition=%wide.region_3.4_spmd, body=%wide.region_2.3_spmd.sunk | while | flops 119542272 | bytes 381037 | solution.py:58
  60.0 3.6 %fusion.23 = f32[4,9,512]{2,1,0:T(8,128)S(1)} fusion(f32[4,9,512]{2,1,0:T(8,128)S(1)} %get-tuple-element.173, s32[]{:T(128)} %get-tuple-element.172, bf16[9,4096]{1,0:T(8,128)(2,1)S(1)} %get-tuple-element.190, bf16[16,4096]{1,0:T(8,128)(2,1)S(1)} %get-tuple-element.187, f32[4096]{0:T(1024)S(1)} %convert_element_type.44, f32[512]{0:T(512)S(1)} %bitcast.53, ...), kind=kOutput, calls=%fused_computation.3.clone.1 | convolution fusion | flops 119537664 | bytes 349184 | tf_op jit(solution)/shard_map/while/body/eval_jaxpr/dot_general | solution.py:54
  63.7 3.6 %fusion.23 = f32[4,9,512]{2,1,0:T(8,128)S(1)} fusion(f32[4,9,512]{2,1,0:T(8,128)S(1)} %get-tuple-element.173, s32[]{:T(128)} %get-tuple-element.172, bf16[9,4096]{1,0:T(8,128)(2,1)S(1)} %get-tuple-element.190, bf16[16,4096]{1,0:T(8,128)(2,1)S(1)} %get-tuple-element.187, f32[4096]{0:T(1024)S(1)} %convert_element_type.44, f32[512]{0:T(512)S(1)} %bitcast.53, ...), kind=kOutput, calls=%fused_computation.3.clone.1 | convolution fusion | flops 119537664 | bytes 349184 | tf_op jit(solution)/shard_map/while/body/eval_jaxpr/dot_general | solution.py:54
  67.3 3.6 %fusion.23 = f32[4,9,512]{2,1,0:T(8,128)S(1)} fusion(f32[4,9,512]{2,1,0:T(8,128)S(1)} %get-tuple-element.173, s32[]{:T(128)} %get-tuple-element.172, bf16[9,4096]{1,0:T(8,128)(2,1)S(1)} %get-tuple-element.190, bf16[16,4096]{1,0:T(8,128)(2,1)S(1)} %get-tuple-element.187, f32[4096]{0:T(1024)S(1)} %convert_element_type.44, f32[512]{0:T(512)S(1)} %bitcast.53, ...), kind=kOutput, calls=%fused_computation.3.clone.1 | convolution fusion | flops 119537664 | bytes 349184 | tf_op jit(solution)/shard_map/while/body/eval_jaxpr/dot_general | solution.py:54
  71.0 3.6 %fusion.23 = f32[4,9,512]{2,1,0:T(8,128)S(1)} fusion(f32[4,9,512]{2,1,0:T(8,128)S(1)} %get-tuple-element.173, s32[]{:T(128)} %get-tuple-element.172, bf16[9,4096]{1,0:T(8,128)(2,1)S(1)} %get-tuple-element.190, bf16[16,4096]{1,0:T(8,128)(2,1)S(1)} %get-tuple-element.187, f32[4096]{0:T(1024)S(1)} %convert_element_type.44, f32[512]{0:T(512)S(1)} %bitcast.53, ...), kind=kOutput, calls=%fused_computation.3.clone.1 | convolution fusion | flops 119537664 | bytes 349184 | tf_op jit(solution)/shard_map/while/body/eval_jaxpr/dot_general | solution.py:54
  74.6 0.1 copy.19
  74.7 0.7 copy.25
  75.4 0.0 reduce-scatter.2.cloned.1.call-update
  75.4 15.6 %reduce-scatter.2.cloned.1.call-done = f32[9,512]{1,0:T(8,128)} async-done(((f32[9,2048]{1,0:T(8,128)}), f32[9,512]{1,0:T(8,128)}) %reduce-scatter.2.cloned.1.call-update) | async-done | bytes 18448 | tf_op jit(solution)/shard_map/reduce_scatter | solution.py:60
  91.0 0.7 slice.19
  91.7 0.7 slice_divide_fusion
  92.4 0.1 multiply_reduce_fusion.1
  92.5 0.1 copy.20
  92.6 42.8 %psum.7 = f32[8,8]{0,1:T(8,128)S(1)} all-reduce(f32[8,8]{0,1:T(8,128)S(1)} %copy.20), channel_id=1, replica_groups=mesh['row'=8,'col'=4] {'row','col'}, use_global_device_ids=true, to_apply=%region_6.7 | all-reduce | flops 64 | bytes 512 | tf_op jit(solution)/shard_map/psum | solution.py:63
  135.4 0.1 copy.21
  135.5 0.7 cholesky.16
  136.2 0.6 compare_reduce_fusion
  136.9 0.6 fusion.10
  137.5 0.6 custom-call.6
  138.1 0.8 convolution_multiply_fusion
  (24 shorter events, 0.3 us)
Async XLA Ops:
  6.5 84.5 %reduce-scatter.2.cloned.1.call-start = ((), (), s32[]{:S(2)}) async-start(), calls=%async_computation.1 | async-start | bytes 163840 | tf_op jit(solution)/shard_map/reduce_scatter | solution.py:60
  29.5 0.7 copy-start.1
  50.2 0.7 copy-start
Sparse Core Ops, SparseCore 0:
  75.5 15.4 reduce-scatter.1
where the time goes:
time: 147 us; the launch traced here: 146 us
  blocking collectives  94.8 us (64%)
  waiting for transfers between devices  15.6 us (11%)
  matrix products  15.2 us (10%)
  between operations  13.5 us (9%)
  other arithmetic  3.67 us (2%)
  local copies, waits for them, and re-layouts  2.89 us (2%)
    psum x1, blocking collectives, shards(): gram = lax.psum(gram_local, ('row', 'col'))  42.8 us
    reduce_scatter x1, waiting for transfers between devices, shards(): total = lax.psum_scatter(row_part, 'col', scatter_dimension=1, tiled=True)  15.6 us
    dot_general x4, matrix products, one_block(): lax.dot_general(col_ext, affinity, (((1,), (1,)), ((), ())), preferred_el...  14.4 us
    all_gather x1, blocking collectives, shards(): lax.all_gather(points, 'col', axis=1, tiled=True)  13.7 us
    all_gather x1, blocking collectives, shards(): lax.all_gather(spread, 'col', axis=0, tiled=True)  11.9 us
    all_gather x1, blocking collectives, shards(): lax.all_gather(points, 'row', axis=1, tiled=True)  9.23 us
    all_gather x1, blocking collectives, shards(): lax.all_gather(vectors, 'row', axis=1, tiled=True)  9.03 us
    all_gather x1, blocking collectives, shards(): lax.all_gather(spread, 'row', axis=0, tiled=True)  8.1 us
  transfers between devices with their start and end apart: 1, of which 1 were waited for; matrix products, arithmetic and copies ran while one was open for 0% of the time, Pallas kernels for 0%

commit v1 on v0

--- a/solution.py
+++ b/solution.py
@@ -60,7 +60,7 @@
     total = lax.psum_scatter(row_part, "col", scatter_dimension=1, tiled=True)
     update = total[:kvec] / total[kvec : kvec + 1]
     gram_local = jnp.sum(update[:, None, :] * update[None, :, :], axis=2)
-    gram = lax.psum(gram_local, ("row", "col"))
+    gram = jnp.sum(lax.all_gather(gram_local, ("row", "col")), axis=0)
     lower = jnp.linalg.cholesky(gram)
     solved = lax.linalg.triangular_solve(lower, update, left_side=True, lower=True)
     count = local * n_row * n_col

time: 147 us -> 172 us (1.17)
  the two profiles are of different devices: /device:TPU:10 before, /device:TPU:0 now
where the time goes in v1:
time: 172 us
  blocking collectives  118 us (69%)
  waiting for transfers between devices  18.5 us (11%)
  matrix products  15.2 us (9%)
  between operations  13.5 us (8%)
  other arithmetic  3.7 us (2%)
  local copies, waits for them, and re-layouts  2.82 us (2%)
    all_gather x1, blocking collectives, shards(): gram = jnp.sum(lax.all_gather(gram_local, ('row', 'col')), axis=0)  64.3 us
    reduce_scatter x1, waiting for transfers between devices, shards(): total = lax.psum_scatter(row_part, 'col', scatter_dimension=1, tiled=True)  18.5 us
    all_gather x1, blocking collectives, shards(): lax.all_gather(points, 'col', axis=1, tiled=True)  15.1 us
    dot_general x4, matrix products, one_block(): lax.dot_general(col_ext, affinity, (((1,), (1,)), ((), ())), preferred_el...  14.4 us
    all_gather x1, blocking collectives, shards(): lax.all_gather(spread, 'col', axis=0, tiled=True)  11.9 us
    all_gather x1, blocking collectives, shards(): lax.all_gather(points, 'row', axis=1, tiled=True)  9.41 us
    all_gather x1, blocking collectives, shards(): lax.all_gather(spread, 'row', axis=0, tiled=True)  8.71 us
    all_gather x1, blocking collectives, shards(): lax.all_gather(vectors, 'row', axis=1, tiled=True)  8.43 us
  transfers between devices with their start and end apart: 1, of which 1 were waited for; matrix products, arithmetic and copies ran while one was open for 0% of the time, Pallas kernels for 0%

profile of v1, /device:TPU:0, one launch (start us, length us, event | category | flops | bytes accessed | tf_op | source)
XLA Modules:
  0.0 171.7 jit_solution(206027055505077796)
XLA Ops:
  6.5 0.0 reduce-scatter.2.cloned.1.call-start
  6.5 15.1 %all_gather.21 = bf16[16,2048]{1,0:T(8,128)(2,1)S(1)} all-gather(bf16[16,512]{1,0:T(8,128)(2,1)} %param.5), channel_id=1, replica_groups=mesh['row'=8,'col'=4] {'col'}, dimensions={1}, use_global_device_ids=true | all-gather | bytes 81920 | tf_op jit(solution)/shard_map/all_gather | solution.py:40
  21.7 9.4 %all_gather.22 = bf16[16,4096]{1,0:T(8,128)(2,1)S(1)} all-gather(bf16[16,512]{1,0:T(8,128)(2,1)} %param.5), channel_id=1, replica_groups=mesh['row'=8,'col'=4] {'row'}, dimensions={1}, use_global_device_ids=true | all-gather | bytes 147456 | tf_op jit(solution)/shard_map/all_gather | solution.py:33
  31.1 0.0 copy-start.1
  31.1 0.6 copy-done.1
  31.8 8.7 %all-gather.2 = bf16[8,1,512]{2,1,0:T(2,128)(2,1)S(1)} all-gather(bf16[1,1,512]{2,1,0:T(2,128)(2,1)S(1)} %reshape.42), channel_id=1, replica_groups=mesh['row'=8,'col'=4] {'row'}, dimensions={0}, use_global_device_ids=true | all-gather | bytes 9216 | tf_op jit(solution)/shard_map/all_gather | solution.py:34
  40.5 11.9 %all-gather.1 = bf16[4,1,512]{2,1,0:T(2,128)(2,1)S(1)} all-gather(bf16[1,1,512]{2,1,0:T(2,128)(2,1)S(1)} %reshape.42), channel_id=1, replica_groups=mesh['row'=8,'col'=4] {'col'}, dimensions={0}, use_global_device_ids=true | all-gather | bytes 5120 | tf_op jit(solution)/shard_map/all_gather | solution.py:41
  52.4 0.0 copy-start
  52.4 0.1 multiply_reduce_fusion
  52.5 0.1 reduce.6
  52.6 0.5 copy-done
  53.1 8.4 %all_gather.25 = bf16[8,4096]{1,0:T(8,128)(2,1)S(1)} all-gather(bf16[8,512]{1,0:T(8,128)(2,1)S(1)} %copy-done), channel_id=1, replica_groups=mesh['row'=8,'col'=4] {'row'}, dimensions={1}, use_global_device_ids=true | all-gather | bytes 73728 | tf_op jit(solution)/shard_map/all_gather | solution.py:35
  61.6 14.6 %while.10 = (s32[]{:T(128)}, f32[4,9,512]{2,1,0:T(8,128)S(1)}, f32[4,512]{1,0:T(4,128)S(1)}, f32[4096]{0:T(1024)S(1)}, bf16[4,16,512]{2,1,0:T(8,128)(2,1)S(1)}, ...) while((s32[]{:T(128)}, f32[4,9,512]{2,1,0:T(8,128)S(1)}, ...), condition=%wide.region_3.4_spmd, body=%wide.region_2.3_spmd.sunk | while | flops 119542272 | bytes 381037 | solution.py:58
  61.6 3.6 %fusion.23 = f32[4,9,512]{2,1,0:T(8,128)S(1)} fusion(f32[4,9,512]{2,1,0:T(8,128)S(1)} %get-tuple-element.173, s32[]{:T(128)} %get-tuple-element.172, bf16[9,4096]{1,0:T(8,128)(2,1)S(1)} %get-tuple-element.190, bf16[16,4096]{1,0:T(8,128)(2,1)S(1)} %get-tuple-element.187, f32[4096]{0:T(1024)S(1)} %convert_element_type.44, f32[512]{0:T(512)S(1)} %bitcast.55, ...), kind=kOutput, calls=%fused_computation.3.clone.1 | convolution fusion | flops 119537664 | bytes 349184 | tf_op jit(solution)/shard_map/while/body/eval_jaxpr/dot_general | solution.py:54
  65.3 3.6 %fusion.23 = f32[4,9,512]{2,1,0:T(8,128)S(1)} fusion(f32[4,9,512]{2,1,0:T(8,128)S(1)} %get-tuple-element.173, s32[]{:T(128)} %get-tuple-element.172, bf16[9,4096]{1,0:T(8,128)(2,1)S(1)} %get-tuple-element.190, bf16[16,4096]{1,0:T(8,128)(2,1)S(1)} %get-tuple-element.187, f32[4096]{0:T(1024)S(1)} %convert_element_type.44, f32[512]{0:T(512)S(1)} %bitcast.55, ...), kind=kOutput, calls=%fused_computation.3.clone.1 | convolution fusion | flops 119537664 | bytes 349184 | tf_op jit(solution)/shard_map/while/body/eval_jaxpr/dot_general | solution.py:54
  68.9 3.6 %fusion.23 = f32[4,9,512]{2,1,0:T(8,128)S(1)} fusion(f32[4,9,512]{2,1,0:T(8,128)S(1)} %get-tuple-element.173, s32[]{:T(128)} %get-tuple-element.172, bf16[9,4096]{1,0:T(8,128)(2,1)S(1)} %get-tuple-element.190, bf16[16,4096]{1,0:T(8,128)(2,1)S(1)} %get-tuple-element.187, f32[4096]{0:T(1024)S(1)} %convert_element_type.44, f32[512]{0:T(512)S(1)} %bitcast.55, ...), kind=kOutput, calls=%fused_computation.3.clone.1 | convolution fusion | flops 119537664 | bytes 349184 | tf_op jit(solution)/shard_map/while/body/eval_jaxpr/dot_general | solution.py:54
  72.5 3.6 %fusion.23 = f32[4,9,512]{2,1,0:T(8,128)S(1)} fusion(f32[4,9,512]{2,1,0:T(8,128)S(1)} %get-tuple-element.173, s32[]{:T(128)} %get-tuple-element.172, bf16[9,4096]{1,0:T(8,128)(2,1)S(1)} %get-tuple-element.190, bf16[16,4096]{1,0:T(8,128)(2,1)S(1)} %get-tuple-element.187, f32[4096]{0:T(1024)S(1)} %convert_element_type.44, f32[512]{0:T(512)S(1)} %bitcast.55, ...), kind=kOutput, calls=%fused_computation.3.clone.1 | convolution fusion | flops 119537664 | bytes 349184 | tf_op jit(solution)/shard_map/while/body/eval_jaxpr/dot_general | solution.py:54
  76.1 0.1 copy.19
  76.2 0.7 copy.26
  76.9 0.0 reduce-scatter.2.cloned.1.call-update
  77.0 18.5 %reduce-scatter.2.cloned.1.call-done = f32[9,512]{1,0:T(8,128)} async-done(((f32[9,2048]{1,0:T(8,128)}), f32[9,512]{1,0:T(8,128)}) %reduce-scatter.2.cloned.1.call-update) | async-done | bytes 18448 | tf_op jit(solution)/shard_map/reduce_scatter | solution.py:60
  95.4 0.7 slice.19
  96.1 0.7 slice_divide_fusion
  96.8 0.1 multiply_reduce_fusion.1
  96.9 64.3 %all-gather = f32[256,8]{1,0:T(8,128)S(1)} all-gather(f32[8,8]{1,0:T(8,128)S(1)} %multiply_reduce_fusion.1), channel_id=2, replica_groups=mesh['row'=8,'col'=4] {'row','col'}, dimensions={0}, use_global_device_ids=true | all-gather | bytes 8448 | tf_op jit(solution)/shard_map/all_gather | solution.py:63
  161.3 0.1 copy.21
  161.4 0.7 cholesky.16
  162.1 0.6 compare_reduce_fusion
  162.8 0.6 fusion.10
  163.5 0.6 custom-call.6
  164.1 0.8 convolution_multiply_fusion
  (25 shorter events, 0.3 us)
Async XLA Ops:
  6.5 88.9 %reduce-scatter.2.cloned.1.call-start = ((), (), s32[]{:S(2)}) async-start(), calls=%async_computation.1 | async-start | bytes 163840 | tf_op jit(solution)/shard_map/reduce_scatter | solution.py:60
  31.1 0.7 copy-start.1
  52.4 0.7 copy-start
Sparse Core Ops, SparseCore 0:
  77.1 18.2 reduce-scatter.1
